TPU v7x, 32 devices: a whole 2x2x4 slice. The times are simulated.
32 devices in a mesh: grp: 2 (over y), rx: 4 (over z), tw: 2 (over x), fq: 2 (over core).
Axes of the slice: x: 2, y: 2, z: 4, core: 2. Of those that a mesh axis runs over, the one named last changes fastest.
Arguments:
- traces: bfloat16 [8, 256, 15360], P('tw', ('grp', 'rx')), parts along dimension 1, may hold values from -48 to 48
- src_index: int32 [8, 64], P('grp'), parts along dimension 0, may hold values from 0 to 127
- valid: int32 [8, 256], P(None, 'grp'), parts along dimension 1, may hold values from 0 to 1, as said below
Outputs:
- correlations: bfloat16 [256, 256, 512], P(('tw', 'fq'), ('grp', 'rx')), parts along dimension 1
There are 2 independent parts, one for each index of `grp`. A program takes and returns all parts, laid end to end along the dimension named above; each array names one. Nothing has to cross between parts.
Inputs may be any that keep to these rules, and one draw needn't show every extreme that they name: `valid`: some channels may be 0 in every window, and some windows 0 on every channel. `src_index`: A channel may be named by several sources.
All inputs are finite; a program needn't handle non-finite values.
Results may differ from a plain program's by a relative error of at most 0.0062.
Values may be sent and summed in bfloat16 or wider, within the bound.
No kernel may reach another device: no remote copies, remote signals or barrier semaphores. Data moves between devices by JAX's collectives and lax.ppermute only.
A program may use at most 128 MiB of HBM per device.

v0:
```python
import math
import jax
import jax.numpy as jnp
from jax import lax
from jax.sharding import PartitionSpec as P

NT = 15360
BAND = 512
F0 = 60
HW = 32
LAGS = 512
two_pi = 2.0 * math.pi
eps_power = 1e-05


def padded_2(block, sides, width):
    for axis, dim in sides:
        count = lax.axis_size(axis)
        forward = [(i, i + 1) for i in range(count - 1)]
        backward = [(target, source) for source, target in forward]
        low = lax.ppermute(
            lax.slice_in_dim(block, block.shape[dim] - width, None, axis=dim), axis, forward
        )
        high = lax.ppermute(lax.slice_in_dim(block, 0, width, axis=dim), axis, backward)
        block = jnp.concatenate([low, block, high], axis=dim)
    return block


def forward_block(row_count, bin_ids, period):
    sample_ids = lax.broadcasted_iota(jnp.int32, (row_count, 1, 1), 0)
    phase_index = sample_ids * bin_ids[None, :, :] % period
    angle_rad = phase_index.astype(jnp.float32) * (two_pi / period)
    coef_block = jnp.stack([jnp.cos(angle_rad), -jnp.sin(angle_rad)], axis=2)
    return coef_block.reshape(row_count, -1).astype(jnp.bfloat16)


def inverse_rows(bin_ids, lag_count, period):
    lag_shift = lax.broadcasted_iota(jnp.int32, (1, lag_count), 1) - lag_count // 2
    phase_index = bin_ids[..., None] * lag_shift % period
    angle_rad = phase_index.astype(jnp.float32) * (two_pi / period)
    return jnp.concatenate([jnp.cos(angle_rad), -jnp.sin(angle_rad)], axis=-2).astype(jnp.bfloat16)


def shards(traces, src_index, valid):
    win_count, chan_count, samples = traces.shape
    tw_count = lax.axis_size("tw")
    fq_count = lax.axis_size("fq")
    tw_pos = lax.axis_index("tw")
    fq_pos = lax.axis_index("fq")
    rx_pos = lax.axis_index("rx")
    band_share = BAND // fq_count
    narrow = band_share // tw_count
    block_len = 1024
    trace_rows = traces.reshape(win_count * chan_count, samples)
    local_bins = (
        F0
        + fq_pos * band_share
        + lax.broadcasted_iota(jnp.int32, (tw_count, narrow), 0) * narrow
        + lax.broadcasted_iota(jnp.int32, (tw_count, narrow), 1)
    )
    base_table = forward_block(block_len, local_bins, samples)

    def accumulate(turn_index, running):
        offset = turn_index * block_len
        trace_piece = lax.dynamic_slice_in_dim(trace_rows, offset, block_len, 1)
        partial_value = jnp.dot(trace_piece, base_table, preferred_element_type=jnp.float32)
        partial_value = partial_value.reshape(-1, tw_count, 2, narrow)
        part_real = partial_value[:, :, 0]
        part_imag = partial_value[:, :, 1]
        phase_index = offset * local_bins % samples
        angle_rad = phase_index.astype(jnp.float32) * (two_pi / samples)
        turn_real = jnp.cos(angle_rad)[None]
        turn_imag = -jnp.sin(angle_rad)[None]
        new_real = part_real * turn_real - part_imag * turn_imag
        new_imag = part_real * turn_imag + part_imag * turn_real
        return running + jnp.stack([new_real, new_imag], axis=2)

    spec_parts = lax.fori_loop(
        0,
        samples // block_len,
        accumulate,
        jnp.zeros((win_count * chan_count, tw_count, 2, narrow), jnp.float32),
    )
    bin_power = (
        spec_parts[:, :, 0] * spec_parts[:, :, 0] + spec_parts[:, :, 1] * spec_parts[:, :, 1]
    )
    bin_power = bin_power.reshape(-1, band_share)
    padded = padded_2(bin_power, (("fq", 1),), HW)
    row_ids = lax.broadcasted_iota(jnp.int32, (band_share + 2 * HW, band_share), 0)
    col_ids = lax.broadcasted_iota(jnp.int32, (band_share + 2 * HW, band_share), 1)
    box_matrix = ((row_ids - col_ids >= 0) & (row_ids - col_ids <= 2 * HW)).astype(jnp.float32)
    smooth = jnp.dot(
        padded, box_matrix, precision=lax.Precision.HIGHEST, preferred_element_type=jnp.float32
    ) / (2 * HW + 1)
    white_gain = lax.rsqrt(smooth + eps_power).reshape(-1, tw_count, 1, narrow)
    whitened = (
        (spec_parts * white_gain)
        .astype(jnp.bfloat16)
        .reshape(win_count, chan_count, tw_count, 2 * narrow)
    )
    valid_float = valid.astype(jnp.float32)
    source_ids = src_index.reshape(-1)
    src_total = source_ids.shape[0]
    channels_all = valid.shape[1]
    pick_all = (
        lax.broadcasted_iota(jnp.int32, (channels_all, src_total), 0) == source_ids[None, :]
    ).astype(jnp.float32)
    source_valid = jnp.dot(
        valid_float, pick_all, precision=lax.Precision.HIGHEST, preferred_element_type=jnp.float32
    )
    receiver_valid = lax.dynamic_slice_in_dim(valid_float, rx_pos * chan_count, chan_count, 1)
    pair_count = jnp.dot(
        source_valid.T,
        receiver_valid,
        precision=lax.Precision.HIGHEST,
        preferred_element_type=jnp.float32,
    )
    pair_floor = jnp.maximum(pair_count, 1.0)[:, :, None]
    pick_local = (
        source_ids[:, None]
        == rx_pos * chan_count + lax.broadcasted_iota(jnp.int32, (1, chan_count), 1)
    ).astype(jnp.bfloat16)
    inv_scale = 1.0 / math.sqrt(BAND)
    own_block = tw_pos * fq_count + fq_pos
    src_local = src_total // (tw_count * fq_count)
    local_terms = jnp.einsum(
        "sc,wcx->swx",
        pick_local,
        whitened.reshape(win_count, chan_count, tw_count * 2 * narrow),
        preferred_element_type=jnp.float32,
    )
    sources = lax.psum(local_terms.astype(jnp.bfloat16), "rx")
    own_sources = lax.all_to_all(
        sources[None], ("tw", "fq"), split_axis=1, concat_axis=0, tiled=True
    )
    all_windows = lax.all_gather(whitened[None], ("tw", "fq"), axis=0, tiled=True)
    src_valid_own = lax.dynamic_slice_in_dim(source_valid, own_block * src_local, src_local, 1)
    src_valid_own = jnp.transpose(src_valid_own.reshape(tw_count, win_count, src_local), (0, 2, 1))
    own_sources = own_sources.reshape(
        tw_count, fq_count, src_local, win_count, tw_count, 2, narrow
    ) * src_valid_own.reshape(tw_count, 1, src_local, win_count, 1, 1, 1).astype(jnp.bfloat16)
    all_windows = all_windows.reshape(
        tw_count, fq_count, win_count, chan_count, tw_count, 2, narrow
    ) * receiver_valid.reshape(tw_count, 1, win_count, chan_count, 1, 1, 1).astype(jnp.bfloat16)
    src_real = own_sources[..., 0, :]
    src_imag = own_sources[..., 1, :]
    rec_real = all_windows[..., 0, :]
    rec_imag = all_windows[..., 1, :]
    pattern = "tfswbx,tfwcbx->scfbx"
    cross_real = jnp.einsum(
        pattern, src_real, rec_real, preferred_element_type=jnp.float32
    ) + jnp.einsum(pattern, src_imag, rec_imag, preferred_element_type=jnp.float32)
    cross_imag = jnp.einsum(
        pattern, src_real, rec_imag, preferred_element_type=jnp.float32
    ) - jnp.einsum(pattern, src_imag, rec_real, preferred_element_type=jnp.float32)
    floor_own = lax.dynamic_slice_in_dim(pair_floor, own_block * src_local, src_local, 0)
    stacked = jnp.concatenate(
        [
            cross_real.reshape(src_local, chan_count, BAND),
            cross_imag.reshape(src_local, chan_count, BAND),
        ],
        axis=2,
    )
    stacked = (stacked / floor_own).astype(jnp.bfloat16)
    inv_table = inverse_rows(F0 + lax.broadcasted_iota(jnp.int32, (BAND,), 0), LAGS, NT)
    summed = jnp.dot(
        stacked.reshape(src_local * chan_count, 2 * BAND),
        inv_table,
        preferred_element_type=jnp.float32,
    ).reshape(src_local, chan_count, LAGS)
    return (summed * inv_scale).astype(jnp.bfloat16)


def solution(mesh):
    return jax.shard_map(
        shards,
        mesh=mesh,
        in_specs=(P("tw", ("grp", "rx"), None), P("grp", None), P(None, "grp")),
        out_specs=P(("tw", "fq"), ("grp", "rx"), None),
        check_vma=False,
    )
```

profile of v0, /device:TPU:0, one launch (start us, length us, event | category | flops | bytes accessed | tf_op | source)
XLA Modules:
  0.0 195.9 jit_solution(17614216192900421187)
XLA Ops:
  6.6 4.6 %cosine_convert_fusion.1 = (bf16[1024,2,1,128]{3,0,2,1:T(8,128)(2,1)S(1)}, bf16[1024,2,1,128]{3,0,2,1:T(8,128)(2,1)S(1)}) fusion(s32[2,128]{1,0:T(2,128)S(1)} %iota_add_fusion.2), kind=kLoop, calls=%fused_computation.47 | loop fusion | flops 3145728 | bytes 1049600 | tf_op jit(solution)/shard_map/convert.2
  12.4 34.7 %while.16 = (s32[]{:T(128)}, f32[128,2,2,128]{3,2,1,0:T(2,128)S(1)}, bf16[128,15360]{1,0:T(8,128)(2,1)}, bf16[1024,512]{1,0:T(8,128)(2,1)S(1)}, s32[2]{0:T(128)S...) while((s32[]{:T(128)}, f32[128,2,2,128]{3,2,1,0:T(2,128)S(1)}, ...), condition=%wide.region_1.2_spmd.clone, body=%wide.region_0.1_spmd.clone.sunk | while | flops 134613760 | bytes 3412133 | solution.py:78
  12.4 1.3 fusion.68
  47.8 2.4 %collective-permute-start = (f32[128,32]{1,0:T(8,128)S(1)}, f32[128,32]{1,0:T(8,128)S(1)}, u32[]{:S(2)}, u32[]{:S(2)}) collective-permute-start(f32[128,32]{1,0:T(8,128)S(1)} %get-tuple-element.179), channel_id=1, source_target_pairs={{0,1},{2,3},{4,5},{6,7},{8,9},{10,11},{12,13},{14,15},{16,17},{18,... | collective-permute-start | bytes 49160 | tf_op jit(solution)/shard_map/ppermute | solution.py:21
  50.2 1.3 collective-permute-start.1
  51.6 1.7 collective-permute-done.1
  54.0 1.5 fusion.14
  56.1 53.5 %all-reduce.2.cloned.1.call-done = bf16[1,256,4,512]{3,1,2,0:T(8,128)(2,1)} async-done(((bf16[1,256,4,512]{3,1,2,0:T(8,128)(2,1)}), bf16[1,256,4,512]{3,1,2,0:T(8,128)(2,1)}) %all-reduce.2.cloned.1.call-update) | async-done | bytes 1048592 | tf_op jit(solution)/shard_map/psum | solution.py:132
  109.7 3.0 %copy.40 = bf16[1,256,4,512]{3,2,0,1:T(4,128)(2,1)} copy(bf16[1,256,4,512]{3,1,2,0:T(8,128)(2,1)} %all-reduce.2.cloned.1.call-done) | data formatting | bytes 2097152 | tf_op jit(solution)/shard_map/psum | solution.py:132
  112.7 4.3 %all-to-all-start = ((bf16[1,256,4,512]{3,2,0,1:T(4,128)(2,1)}), bf16[1,256,4,512]{3,2,0,1:T(4,128)(2,1)}, u32[]{:S(2)}, u32[]{:S(2)}) async-start(bf16[1,256,4,512]{3,2,0,1:T(4,128)(2,1)} %copy.40), calls=%async_computation | async-start | bytes 2097152 | tf_op jit(solution)/shard_map/all_to_all | solution.py:133
  117.1 5.7 %cosine_convert_fusion = (bf16[512,512]{1,0:T(8,128)(2,1)}, bf16[512,512]{1,0:T(8,128)(2,1)}) fusion(s32[512]{0:T(512)S(1)} %get-tuple-element.185, s32[512]{0:T(512)S(1)} %get-tuple-element.186), kind=kLoop, calls=%fused_computation.40 | loop fusion | flops 3145728 | bytes 1052672 | tf_op jit(solution)/shard_map/convert
  123.0 12.0 %all_gather.3 = bf16[4,4,32,2,256]{4,2,3,1,0:T(8,128)(2,1)S(1)} all-gather(bf16[1,4,32,2,256]{4,2,3,1,0:T(8,128)(2,1)S(1)} %copy.38), channel_id=1, replica_groups=mesh['grp'=2,'rx'=4,'tw'=2,'fq'=2] {'tw','fq'}, dimensions={0}, use_global_device_ids=true | all-gather | bytes 655360 | tf_op jit(solution)/shard_map/all_gather | solution.py:136
  135.1 2.5 %copy.39 = bf16[2,2,4,32,2,2,128]{3,2,0,6,4,1,5:T(4,128)(2,1)} copy(bf16[2,2,4,32,2,2,128]{6,5,3,4,2,1,0:T(2,128)(2,1)S(1)} %reshape.161) | data formatting | bytes 1048576 | tf_op jit(solution)/shard_map/reshape | solution.py:142
  137.7 1.7 broadcast_multiply_fusion.1
  139.4 1.5 reshape.171
  140.9 4.3 %copy.42 = bf16[2,2,64,4,2,2,128]{2,3,0,6,4,1,5:T(4,128)(2,1)} copy(bf16[2,2,64,4,2,2,128]{6,5,4,3,2,1,0:T(2,128)(2,1)S(1)} %reshape.171) | data formatting | bytes 2097152 | tf_op jit(solution)/shard_map/reshape | solution.py:139
  145.1 1.7 broadcast_multiply_fusion
  146.9 1.8 fusion.29
  148.7 4.2 %fusion.30 = f32[2,2,128,32,64,1]{4,3,5,2,1,0:T(8,128)} fusion(bf16[2,2,64,4,2,2,128]{2,3,0,6,4,1,5:T(4,128)(2,1)S(1)} %bitcast.78, bf16[2,2,4,32,2,2,128]{3,2,0,6,4,1,5:T(4,128)(2,1)S(1)} %bitcast.74), kind=kOutput, calls=%fused_computation.54 | convolution fusion | flops 16777216 | bytes 6291456 | tf_op jit(solution)/shard_map/tfswbx,tfwcbx->scfbx/dot_general | solution.py:153
  152.9 4.3 %bitcast_add_fusion = f32[2,2,128,32,64]{4,3,2,1,0:T(8,128)} fusion(f32[2,2,128,32,64,1]{4,3,5,2,1,0:T(8,128)S(1)} %fusion.29, bf16[2,2,4,32,2,2,128]{3,2,0,6,4,1,5:T(4,128)(2,1)S(1)} %bitcast.75, bf16[2,2,64,4,2,2,128]{2,3,0,6,4,1,5:T(4,128)(2,1)S(1)} %bitcast.79), kind=kOutput, calls=%fused_computation.17 | convolution fusion | flops 17825792 | bytes 14680064 | tf_op jit(solution)/shard_map/tfswbx,tfwcbx->scfbx/dot_general | solution.py:152
  157.2 7.7 %copy.43 = f32[64,32,512]{2,1,0:T(8,128)} copy(f32[64,32,512]{0,1,2:T(8,128)} %bitcast.72) | data formatting | bytes 8388608 | tf_op jit(solution)/shard_map/concatenate | solution.py:157
  165.0 9.1 %bitcast_subtract_fusion = f32[2,2,128,32,64]{4,3,2,1,0:T(8,128)} fusion(f32[2,2,128,32,64,1]{4,3,5,2,1,0:T(8,128)} %fusion.30, bf16[2,2,4,32,2,2,128]{3,2,0,6,4,1,5:T(4,128)(2,1)S(1)} %bitcast.76, bf16[2,2,64,4,2,2,128]{2,3,0,6,4,1,5:T(4,128)(2,1)} %bitcast.80), kind=kOutput, calls=%fused_computation.16 | convolution fusion | flops 17825792 | bytes 14680064 | tf_op jit(solution)/shard_map/tfswbx,tfwcbx->scfbx/dot_general | solution.py:155
  174.0 7.8 %copy.44 = f32[64,32,512]{2,1,0:T(8,128)} copy(f32[64,32,512]{0,1,2:T(8,128)} %bitcast.71) | data formatting | bytes 8388608 | tf_op jit(solution)/shard_map/concatenate | solution.py:157
  181.8 7.2 %multiply_convert_fusion = bf16[64,32,512]{2,1,0:T(8,128)(2,1)} fusion(f32[64,32,512]{2,1,0:T(8,128)} %copy.44, f32[64,32,512]{2,1,0:T(8,128)} %copy.43, f32[64,32]{1,0:T(8,128)S(1)} %copy.45, bf16[512,512]{1,0:T(8,128)(2,1)S(1)} %copy-done.2, bf16[512,512]{1,0:T(8,128)(2,1)S(1)} %copy-done.1), kind=kOutput, calls=%fused_computation.18 | convolution fusion | flops 2157969408 | bytes 11542528 | tf_op jit(solution)/shard_map/dot_general | solution.py:166
  (114 shorter events, 36.5 us)
Async XLA Ops:
  6.5 103.1 %all-reduce.2.cloned.1.call-start = ((), (), s32[]{:S(2)}) async-start(), calls=%async_computation.1 | async-start | bytes 2097152 | tf_op jit(solution)/shard_map/psum | solution.py:132
  12.4 39.1 %copy-start.4 = (s32[4,64]{1,0:T(4,128)S(1)}, s32[4,64]{1,0:T(4,128)}, u32[]{:S(2)}) copy-start(s32[4,64]{1,0:T(4,128)} %param.6) | copy-start | bytes 3076
  47.7 7.8 %copy-start.3 = (s32[8,128]{1,0:T(8,128)S(1)}, s32[8,128]{1,0:T(8,128)}, u32[]{:S(2)}) copy-start(s32[8,128]{1,0:T(8,128)} %param.7) | copy-start | bytes 12292
  47.8 3.8 %collective-permute-start = (f32[128,32]{1,0:T(8,128)S(1)}, f32[128,32]{1,0:T(8,128)S(1)}, u32[]{:S(2)}, u32[]{:S(2)}) collective-permute-start(f32[128,32]{1,0:T(8,128)S(1)} %get-tuple-element.179), channel_id=1, source_target_pairs={{0,1},{2,3},{4,5},{6,7},{8,9},{10,11},{12,13},{14,15},{16,17},{18,... | collective-permute-start | bytes 49160 | tf_op jit(solution)/shard_map/ppermute | solution.py:21
  50.2 3.1 %collective-permute-start.1 = (f32[128,32]{1,0:T(8,128)S(1)}, f32[128,32]{1,0:T(8,128)S(1)}, u32[]{:S(2)}, u32[]{:S(2)}) collective-permute-start(f32[128,32]{1,0:T(8,128)S(1)} %get-tuple-element.180), channel_id=1, source_target_pairs={{1,0},{3,2},{5,4},{7,6},{9,8},{11,10},{13,12},{15,14},{17,16},{19,... | collective-permute-start | bytes 49160 | tf_op jit(solution)/shard_map/ppermute | solution.py:24
  112.7 26.7 %all-to-all-start = ((bf16[1,256,4,512]{3,2,0,1:T(4,128)(2,1)}), bf16[1,256,4,512]{3,2,0,1:T(4,128)(2,1)}, u32[]{:S(2)}, u32[]{:S(2)}) async-start(bf16[1,256,4,512]{3,2,0,1:T(4,128)(2,1)} %copy.40), calls=%async_computation | async-start | bytes 2097152 | tf_op jit(solution)/shard_map/all_to_all | solution.py:133
  146.9 6.0 %copy-start = (bf16[1,2,64,8,2,2,128]{2,3,0,6,4,1,5:T(8,128)(2,1)}, bf16[1,2,64,8,2,2,128]{2,3,0,6,4,1,5:T(8,128)(2,1)S(1)}, u32[]{:S(2)}) copy-start(bf16[1,2,64,8,2,2,128]{2,3,0,6,4,1,5:T(8,128)(2,1)S(1)} %broadcast_multiply_fusion) | copy-start | bytes 3145732
  174.0 7.8 %copy-start.1 = (bf16[512,512]{1,0:T(8,128)(2,1)S(1)}, bf16[512,512]{1,0:T(8,128)(2,1)}, u32[]{:S(2)}) copy-start(bf16[512,512]{1,0:T(8,128)(2,1)} %get-tuple-element.181) | copy-start | bytes 1572868
  174.0 7.8 %copy-start.2 = (bf16[512,512]{1,0:T(8,128)(2,1)S(1)}, bf16[512,512]{1,0:T(8,128)(2,1)}, u32[]{:S(2)}) copy-start(bf16[512,512]{1,0:T(8,128)(2,1)} %get-tuple-element.182) | copy-start | bytes 1572868
Sparse Core Ops, SparseCore 0:
  55.6 54.0 all-reduce.1
where the time goes:
time: 197 us; the launch traced here: 196 us
  waiting for transfers between devices  55.3 us (28%)
  matrix products  47.8 us (24%)
  local copies, waits for them, and re-layouts  31.2 us (16%)
  other arithmetic  27.4 us (14%)
  between operations  13.6 us (7%)
  blocking collectives  12 us (6%)
  starting transfers between devices  7.95 us (4%)
    psum x1, waiting for transfers between devices, shards(): sources = lax.psum(local_terms.astype(jnp.bfloat16), 'rx')  53.5 us
    dot_general x15, matrix products, accumulate(): jnp.dot(trace_piece, base_table, preferred_element_type=jnp.float32)  18.9 us
    concatenate x2, local copies, waits for them, and re-layouts, shards(): jnp.concatenate([cross_real.reshape(src_local, chan_count, BAND), cross_i...  15.5 us
    all_gather x1, blocking collectives, shards(): lax.all_gather(whitened[None], ('tw', 'fq'), axis=0, tiled=True)  12 us
    another operation x2, other arithmetic  10.3 us
    dot_general x1, matrix products, shards(): jnp.einsum(pattern, src_imag, rec_real, preferred_element_type=jnp.float32)  9.08 us
    dot_general x1, matrix products, shards(): jnp.dot(stacked.reshape(src_local * chan_count, 2 * BAND), inv_table, pre...  7.22 us
    add x15, other arithmetic, accumulate(): return running + jnp.stack([new_real, new_imag], axis=2)  6.72 us
  transfers between devices with their start and end apart: 4, of which 2 were waited for; matrix products, arithmetic and copies ran while one was open for 6% of the time, Pallas kernels for 0%

commit v1 on v0

--- a/solution.py
+++ b/solution.py
@@ -133,7 +133,12 @@
     own_sources = lax.all_to_all(
         sources[None], ("tw", "fq"), split_axis=1, concat_axis=0, tiled=True
     )
-    all_windows = lax.all_gather(whitened[None], ("tw", "fq"), axis=0, tiled=True)
+    all_windows = jnp.concatenate(
+        lax.all_to_all(
+            jnp.stack([whitened[None]] * lax.axis_size(("tw", "fq"))), ("tw", "fq"), 0, 0
+        ),
+        axis=0,
+    )
     src_valid_own = lax.dynamic_slice_in_dim(source_valid, own_block * src_local, src_local, 1)
     src_valid_own = jnp.transpose(src_valid_own.reshape(tw_count, win_count, src_local), (0, 2, 1))
     own_sources = own_sources.reshape(

time: 197 us -> 189 us (0.959)
  blocking collectives: 12 us -> 0 us
  starting transfers between devices: 7.95 us -> 11.7 us
    all_gather x1 -> x0, blocking collectives: 12 us -> none  [shards(): lax.all_gather(whitened[None], ('tw', 'fq'), axis=0, tiled=True)]
    psum x1, waiting for transfers between devices: 53.5 us -> 48.8 us  [shards(): sources = lax.psum(local_terms.astype(jnp.bfloat16), 'rx')]
    all_to_all x1, waiting for transfers between devices: 0.01 us -> 4.12 us  [shards(): lax.all_to_all(sources[None], ('tw', 'fq'), split_axis=1, concat_axis=0,...]
    all_to_all x0 -> x1, starting transfers between devices: none -> 3.6 us  [shards(): lax.all_to_all(jnp.stack([whitened[None]] * lax.axis_size(('tw', 'fq'))),...]
    another operation x3 -> x6, local copies, waits for them, and re-layouts: 0.18 us -> 3.74 us  [the longest x2 2.66 us: shards(): all_windows.reshape(tw_count, fq_count, win_count, chan_count, tw_count,...]
    reshape x2 -> x0, local copies, waits for them, and re-layouts: 2.66 us -> none  [shards(): all_windows.reshape(tw_count, fq_count, win_count, chan_count, tw_count,...]
  transfers between devices with their start and end apart: 4 -> 5, of which waited for: 2 -> 3; matrix products, arithmetic and copies ran while one was open for 6% -> 8% of each run, Pallas kernels for 0% -> 0%
where the time goes in v1:
time: 189 us; the launch traced here: 188 us
  waiting for transfers between devices  54.7 us (29%)
  matrix products  47.7 us (25%)
  local copies, waits for them, and re-layouts  32 us (17%)
  other arithmetic  27.4 us (14%)
  between operations  13.6 us (7%)
  starting transfers between devices  11.7 us (6%)
    psum x1, waiting for transfers between devices, shards(): sources = lax.psum(local_terms.astype(jnp.bfloat16), 'rx')  48.8 us
    dot_general x15, matrix products, accumulate(): jnp.dot(trace_piece, base_table, preferred_element_type=jnp.float32)  18.9 us
    concatenate x2, local copies, waits for them, and re-layouts, shards(): jnp.concatenate([cross_real.reshape(src_local, chan_count, BAND), cross_i...  15.4 us
    another operation x2, other arithmetic  10.3 us
    dot_general x1, matrix products, shards(): jnp.einsum(pattern, src_imag, rec_real, preferred_element_type=jnp.float32)  9.07 us
    dot_general x1, matrix products, shards(): jnp.dot(stacked.reshape(src_local * chan_count, 2 * BAND), inv_table, pre...  7.22 us
    add x15, other arithmetic, accumulate(): return running + jnp.stack([new_real, new_imag], axis=2)  6.72 us
    reshape x2, local copies, waits for them, and re-layouts, shards(): own_sources.reshape(tw_count, fq_count, src_local, win_count, tw_count, 2...  5.72 us
  transfers between devices with their start and end apart: 5, of which 3 were waited for; matrix products, arithmetic and copies ran while one was open for 8% of the time, Pallas kernels for 0%

profile of v1, /device:TPU:0, one launch (start us, length us, event | category | flops | bytes accessed | tf_op | source)
XLA Modules:
  0.0 187.8 jit_solution(7708293239737642877)
XLA Ops:
  6.6 4.6 %cosine_convert_fusion.1 = (bf16[1024,2,1,128]{3,0,2,1:T(8,128)(2,1)S(1)}, bf16[1024,2,1,128]{3,0,2,1:T(8,128)(2,1)S(1)}) fusion(s32[2,128]{1,0:T(2,128)S(1)} %iota_add_fusion.2), kind=kLoop, calls=%fused_computation.47 | loop fusion | flops 3145728 | bytes 1049600 | tf_op jit(solution)/shard_map/convert.2
  12.4 34.7 %while.16 = (s32[]{:T(128)}, f32[128,2,2,128]{3,2,1,0:T(2,128)S(1)}, bf16[128,15360]{1,0:T(8,128)(2,1)}, bf16[1024,512]{1,0:T(8,128)(2,1)S(1)}, s32[2]{0:T(128)S...) while((s32[]{:T(128)}, f32[128,2,2,128]{3,2,1,0:T(2,128)S(1)}, ...), condition=%wide.region_1.2_spmd.clone, body=%wide.region_0.1_spmd.clone.sunk | while | flops 134613760 | bytes 3412133 | solution.py:78
  47.8 2.4 %collective-permute-start = (f32[128,32]{1,0:T(8,128)S(1)}, f32[128,32]{1,0:T(8,128)S(1)}, u32[]{:S(2)}, u32[]{:S(2)}) collective-permute-start(f32[128,32]{1,0:T(8,128)S(1)} %get-tuple-element.179), channel_id=1, source_target_pairs={{0,1},{2,3},{4,5},{6,7},{8,9},{10,11},{12,13},{14,15},{16,17},{18,... | collective-permute-start | bytes 49160 | tf_op jit(solution)/shard_map/ppermute | solution.py:21
  50.2 1.3 collective-permute-start.1
  51.6 1.7 collective-permute-done.1
  54.0 1.5 fusion.14
  56.7 3.6 %all-to-all-start = ((bf16[4,1,4,32,2,256]{5,3,4,2,1,0:T(8,128)(2,1)}), bf16[4,1,4,32,2,256]{5,3,4,2,1,0:T(8,128)(2,1)S(1)}, u32[]{:S(2)}, u32[]{:S(2)}) async-start(bf16[4,1,4,32,2,256]{5,3,4,2,1,0:T(8,128)(2,1)} %stack.26), calls=%async_computation | async-start | bytes 1048576 | tf_op jit(solution)/shard_map/all_to_all | solution.py:137
  60.8 48.8 %all-reduce.2.cloned.1.call-done = bf16[1,256,4,512]{3,1,2,0:T(8,128)(2,1)} async-done(((bf16[1,256,4,512]{3,1,2,0:T(8,128)(2,1)}), bf16[1,256,4,512]{3,1,2,0:T(8,128)(2,1)}) %all-reduce.2.cloned.1.call-update) | async-done | bytes 1048592 | tf_op jit(solution)/shard_map/psum | solution.py:132
  109.6 3.0 %copy.38 = bf16[1,256,4,512]{3,2,0,1:T(4,128)(2,1)} copy(bf16[1,256,4,512]{3,1,2,0:T(8,128)(2,1)} %all-reduce.2.cloned.1.call-done) | data formatting | bytes 2097152 | tf_op jit(solution)/shard_map/psum | solution.py:132
  112.6 4.4 %all-to-all-start.1 = ((bf16[1,256,4,512]{3,2,0,1:T(4,128)(2,1)}), bf16[1,256,4,512]{3,2,0,1:T(4,128)(2,1)}, u32[]{:S(2)}, u32[]{:S(2)}) async-start(bf16[1,256,4,512]{3,2,0,1:T(4,128)(2,1)} %copy.38), calls=%async_computation.1 | async-start | bytes 2097152 | tf_op jit(solution)/shard_map/all_to_all | solution.py:133
  117.2 5.7 %cosine_convert_fusion = (bf16[512,512]{1,0:T(8,128)(2,1)}, bf16[512,512]{1,0:T(8,128)(2,1)}) fusion(s32[512]{0:T(512)S(1)} %get-tuple-element.185, s32[512]{0:T(512)S(1)} %get-tuple-element.186), kind=kLoop, calls=%fused_computation.40 | loop fusion | flops 3145728 | bytes 1052672 | tf_op jit(solution)/shard_map/convert
  123.0 2.5 %copy.37 = bf16[2,2,4,32,2,2,128]{3,2,0,6,4,1,5:T(4,128)(2,1)} copy(bf16[2,2,4,32,2,2,128]{6,5,3,4,2,1,0:T(2,128)(2,1)S(1)} %reshape_reshape.6) | data formatting | bytes 1048576 | tf_op jit(solution)/shard_map/reshape;reshape | solution.py:147
  125.5 1.7 broadcast_multiply_fusion.1
  127.3 4.1 %all-to-all-done.1 = bf16[1,256,4,512]{3,2,0,1:T(4,128)(2,1)} async-done(((bf16[1,256,4,512]{3,2,0,1:T(4,128)(2,1)}), bf16[1,256,4,512]{3,2,0,1:T(4,128)(2,1)}, u32[]{:S(2)}, u32[]{:S(2)}) %all-to-all-start.1) | async-done | bytes 1048608 | tf_op jit(solution)/shard_map/all_to_all | solution.py:133
  131.4 1.5 reshape.170
  132.9 4.3 %copy.40 = bf16[2,2,64,4,2,2,128]{2,3,0,6,4,1,5:T(4,128)(2,1)} copy(bf16[2,2,64,4,2,2,128]{6,5,4,3,2,1,0:T(2,128)(2,1)S(1)} %reshape.170) | data formatting | bytes 2097152 | tf_op jit(solution)/shard_map/reshape | solution.py:144
  137.1 1.7 broadcast_multiply_fusion
  138.9 1.8 fusion.29
  140.6 4.2 %fusion.30 = f32[2,2,128,32,64,1]{4,3,5,2,1,0:T(8,128)} fusion(bf16[2,2,64,4,2,2,128]{2,3,0,6,4,1,5:T(4,128)(2,1)S(1)} %bitcast.78, bf16[2,2,4,32,2,2,128]{3,2,0,6,4,1,5:T(4,128)(2,1)S(1)} %bitcast.74), kind=kOutput, calls=%fused_computation.54 | convolution fusion | flops 16777216 | bytes 6291456 | tf_op jit(solution)/shard_map/tfswbx,tfwcbx->scfbx/dot_general | solution.py:158
  144.8 4.4 %bitcast_add_fusion = f32[2,2,128,32,64]{4,3,2,1,0:T(8,128)} fusion(f32[2,2,128,32,64,1]{4,3,5,2,1,0:T(8,128)S(1)} %fusion.29, bf16[2,2,4,32,2,2,128]{3,2,0,6,4,1,5:T(4,128)(2,1)S(1)} %bitcast.75, bf16[2,2,64,4,2,2,128]{2,3,0,6,4,1,5:T(4,128)(2,1)S(1)} %bitcast.79), kind=kOutput, calls=%fused_computation.17 | convolution fusion | flops 17825792 | bytes 14680064 | tf_op jit(solution)/shard_map/tfswbx,tfwcbx->scfbx/dot_general | solution.py:157
  149.2 7.7 %copy.41 = f32[64,32,512]{2,1,0:T(8,128)} copy(f32[64,32,512]{0,1,2:T(8,128)} %bitcast.72) | data formatting | bytes 8388608 | tf_op jit(solution)/shard_map/concatenate | solution.py:162
  156.8 9.1 %bitcast_subtract_fusion = f32[2,2,128,32,64]{4,3,2,1,0:T(8,128)} fusion(f32[2,2,128,32,64,1]{4,3,5,2,1,0:T(8,128)} %fusion.30, bf16[2,2,4,32,2,2,128]{3,2,0,6,4,1,5:T(4,128)(2,1)S(1)} %bitcast.76, bf16[2,2,64,4,2,2,128]{2,3,0,6,4,1,5:T(4,128)(2,1)} %bitcast.80), kind=kOutput, calls=%fused_computation.16 | convolution fusion | flops 17825792 | bytes 14680064 | tf_op jit(solution)/shard_map/tfswbx,tfwcbx->scfbx/dot_general | solution.py:160
  165.9 7.8 %copy.42 = f32[64,32,512]{2,1,0:T(8,128)} copy(f32[64,32,512]{0,1,2:T(8,128)} %bitcast.71) | data formatting | bytes 8388608 | tf_op jit(solution)/shard_map/concatenate | solution.py:162
  173.7 7.2 %multiply_convert_fusion = bf16[64,32,512]{2,1,0:T(8,128)(2,1)} fusion(f32[64,32,512]{2,1,0:T(8,128)} %copy.42, f32[64,32,512]{2,1,0:T(8,128)} %copy.41, f32[64,32]{1,0:T(8,128)S(1)} %copy.43, bf16[512,512]{1,0:T(8,128)(2,1)S(1)} %copy-done.2, bf16[512,512]{1,0:T(8,128)(2,1)S(1)} %copy-done.1), kind=kOutput, calls=%fused_computation.18 | convolution fusion | flops 2157969408 | bytes 11542528 | tf_op jit(solution)/shard_map/dot_general | solution.py:171
  (116 shorter events, 38.6 us)
Async XLA Ops:
  6.5 103.1 %all-reduce.2.cloned.1.call-start = ((), (), s32[]{:S(2)}) async-start(), calls=%async_computation.2 | async-start | bytes 2097152 | tf_op jit(solution)/shard_map/psum | solution.py:132
  12.4 39.1 %copy-start.4 = (s32[4,64]{1,0:T(4,128)S(1)}, s32[4,64]{1,0:T(4,128)}, u32[]{:S(2)}) copy-start(s32[4,64]{1,0:T(4,128)} %param.6) | copy-start | bytes 3076
  47.7 7.8 %copy-start.3 = (s32[8,128]{1,0:T(8,128)S(1)}, s32[8,128]{1,0:T(8,128)}, u32[]{:S(2)}) copy-start(s32[8,128]{1,0:T(8,128)} %param.7) | copy-start | bytes 12292
  47.8 3.8 %collective-permute-start = (f32[128,32]{1,0:T(8,128)S(1)}, f32[128,32]{1,0:T(8,128)S(1)}, u32[]{:S(2)}, u32[]{:S(2)}) collective-permute-start(f32[128,32]{1,0:T(8,128)S(1)} %get-tuple-element.179), channel_id=1, source_target_pairs={{0,1},{2,3},{4,5},{6,7},{8,9},{10,11},{12,13},{14,15},{16,17},{18,... | collective-permute-start | bytes 49160 | tf_op jit(solution)/shard_map/ppermute | solution.py:21
  50.2 3.1 %collective-permute-start.1 = (f32[128,32]{1,0:T(8,128)S(1)}, f32[128,32]{1,0:T(8,128)S(1)}, u32[]{:S(2)}, u32[]{:S(2)}) collective-permute-start(f32[128,32]{1,0:T(8,128)S(1)} %get-tuple-element.180), channel_id=1, source_target_pairs={{1,0},{3,2},{5,4},{7,6},{9,8},{11,10},{13,12},{15,14},{17,16},{19,... | collective-permute-start | bytes 49160 | tf_op jit(solution)/shard_map/ppermute | solution.py:24
  56.7 56.0 %all-to-all-start = ((bf16[4,1,4,32,2,256]{5,3,4,2,1,0:T(8,128)(2,1)}), bf16[4,1,4,32,2,256]{5,3,4,2,1,0:T(8,128)(2,1)S(1)}, u32[]{:S(2)}, u32[]{:S(2)}) async-start(bf16[4,1,4,32,2,256]{5,3,4,2,1,0:T(8,128)(2,1)} %stack.26), calls=%async_computation | async-start | bytes 1048576 | tf_op jit(solution)/shard_map/all_to_all | solution.py:137
  112.6 18.8 %all-to-all-start.1 = ((bf16[1,256,4,512]{3,2,0,1:T(4,128)(2,1)}), bf16[1,256,4,512]{3,2,0,1:T(4,128)(2,1)}, u32[]{:S(2)}, u32[]{:S(2)}) async-start(bf16[1,256,4,512]{3,2,0,1:T(4,128)(2,1)} %copy.38), calls=%async_computation.1 | async-start | bytes 2097152 | tf_op jit(solution)/shard_map/all_to_all | solution.py:133
  138.9 6.0 %copy-start = (bf16[1,2,64,8,2,2,128]{2,3,0,6,4,1,5:T(8,128)(2,1)}, bf16[1,2,64,8,2,2,128]{2,3,0,6,4,1,5:T(8,128)(2,1)S(1)}, u32[]{:S(2)}) copy-start(bf16[1,2,64,8,2,2,128]{2,3,0,6,4,1,5:T(8,128)(2,1)S(1)} %broadcast_multiply_fusion) | copy-start | bytes 3145732
  165.9 7.8 %copy-start.1 = (bf16[512,512]{1,0:T(8,128)(2,1)S(1)}, bf16[512,512]{1,0:T(8,128)(2,1)}, u32[]{:S(2)}) copy-start(bf16[512,512]{1,0:T(8,128)(2,1)} %get-tuple-element.181) | copy-start | bytes 1572868
  165.9 7.8 %copy-start.2 = (bf16[512,512]{1,0:T(8,128)(2,1)S(1)}, bf16[512,512]{1,0:T(8,128)(2,1)}, u32[]{:S(2)}) copy-start(bf16[512,512]{1,0:T(8,128)(2,1)} %get-tuple-element.182) | copy-start | bytes 1572868
Sparse Core Ops, SparseCore 0:
  55.6 53.9 all-reduce.1
